TPU v7x, 32 devices: a whole 2x2x4 slice. The times are simulated.
32 devices in a mesh: dp: 16 (over z, y, core), mp: 2 (over x).
Axes of the slice: x: 2, y: 2, z: 4, core: 2. Of those that a mesh axis runs over, the one named last changes fastest.
Arguments:
- hidden_in: bfloat16 [8192, 4096], P('dp'), may hold values from -1.5 to 1.5
- w_query: bfloat16 [4096, 4096], P('dp', 'mp'), may hold values from -1 to 1
- w_key: bfloat16 [4096, 1024], P('dp', 'mp'), may hold values from -24 to 24
- w_value: bfloat16 [4096, 1024], P('dp', 'mp'), may hold values from -1 to 1
- w_out: bfloat16 [4096, 4096], P('dp', 'mp'), may hold values from -1 to 1
- value_weight: float32 [4096], P('mp'), may hold values from -0.09375 to 0.09375
- rewards: float32 [8192], P('dp'), may hold values from -0.6 to 0.6
- old_values: float32 [8192], P('dp'), may hold values from -6 to 6
- lengths: int32 [64], replicated, may hold values from 1 to 2048, 8192 in all
- terminal: int32 [64], replicated, may hold values 0 or 1
Outputs:
- value: float32 [8192], P('dp')
- advantage: float32 [8192], P('dp')
- value_loss: float32 [], replicated
All inputs are finite; a program needn't handle non-finite values.
Results may differ from a plain program's by a relative error of at most 0.012.
The roundings to bfloat16 on the way count: a program that leaves them out, or rounds other values in their place, can miss the bound.
Values may be sent and summed in bfloat16 or wider, within the bound.
No kernel may reach another device: no remote copies, remote signals or barrier semaphores. Data moves between devices by JAX's collectives and lax.ppermute only.
A program may use at most 128 MiB of HBM per device.

v0:
```python
import jax
import jax.numpy as jnp
from jax import lax
from jax.sharding import PartitionSpec as P

HEAD = 128
discount = 0.999
trace_decay = 0.997
clip_range = 0.2
epsilon = 1e-05
rope_base = 500000.0


def from_behind(array, axis, by):
    size = lax.axis_size(axis)
    pairs = [(i, i + by) for i in range(size) if 0 <= i + by < size]
    return lax.ppermute(array, axis, pairs)


def carried_in(part, axis, combine, identity):
    count = lax.axis_size(axis)
    place = lax.axis_index(axis)
    ahead = count - 1 - place
    gathered = jax.tree.map(lambda a: lax.all_gather(a, axis), part)
    state = jax.tree.map(lambda a, e: jnp.zeros_like(a) + jnp.asarray(e, a.dtype), part, identity)

    def one(hop, state):
        source = count - 1 - hop
        return combine(
            state, jax.tree.map(lambda a: lax.dynamic_index_in_dim(a, source, 0, False), gathered)
        )

    return lax.fori_loop(0, ahead, one, state)


def rotate(states, positions):
    half = HEAD // 2
    freq = rope_base ** (-jnp.arange(half, dtype=jnp.float32) * 2.0 / HEAD)
    angles = positions[:, None] * freq[None, :]
    cosine = jnp.cos(angles)[:, None, :]
    sine = jnp.sin(angles)[:, None, :]
    first = states[..., :half]
    second = states[..., half:]
    return jnp.concatenate([first * cosine - second * sine, second * cosine + first * sine], -1)


def body(
    hidden_in, w_query, w_key, w_value, w_out, value_weight, rewards, old_values, lengths, terminal
):
    rows = hidden_in.shape[0]
    width = hidden_in.shape[1]
    states = hidden_in.astype(jnp.float32)
    normed = (states * lax.rsqrt(jnp.mean(states * states, 1, keepdims=True) + epsilon)).astype(
        jnp.bfloat16
    )
    pieces = (
        lax.all_gather(w_query, "dp", axis=0, tiled=True),
        lax.all_gather(w_key, "dp", axis=0, tiled=True),
        lax.all_gather(w_value, "dp", axis=0, tiled=True),
        lax.all_gather(w_out, "dp", axis=0, tiled=True),
    )
    add_pieces = pieces[:3]
    summed = tuple(
        (jnp.dot(normed, piece, preferred_element_type=jnp.float32) for piece in add_pieces)
    )
    stored = pieces[3]
    query_sum, key_sum, value_sum, whole_out = summed + (stored,)
    position_ids = lax.axis_index("dp") * rows + jnp.arange(rows, dtype=jnp.int32)
    positions = position_ids.astype(jnp.float32)
    local_heads = w_query.shape[1] // HEAD
    local_kv = w_key.shape[1] // HEAD
    group = local_heads // local_kv
    query = rotate(query_sum.reshape(rows, local_heads, HEAD), positions).astype(jnp.bfloat16)
    key = rotate(key_sum.reshape(rows, local_kv, HEAD), positions).astype(jnp.bfloat16)
    values_proj = value_sum.astype(jnp.bfloat16).reshape(rows, local_kv, HEAD)
    ends = jnp.cumsum(lengths)
    matches = ends[None, :] - 1 == position_ids[:, None]
    finished = jnp.any(matches, 1).astype(jnp.float32)
    stopped = jnp.sum(jnp.where(matches, terminal[None, :], 0), 1).astype(jnp.float32)
    episode = jnp.sum((ends[None, :] <= position_ids[:, None]).astype(jnp.int32), 1)
    order = jnp.arange(rows, dtype=jnp.int32)
    same_episode = episode[None, :] == episode[:, None]
    allowed = (order[None, :] <= order[:, None]) & same_episode
    scores = jnp.einsum(
        "tkgd,skd->kgts",
        query.reshape(rows, local_kv, group, HEAD),
        key,
        preferred_element_type=jnp.float32,
    ) * (1.0 / HEAD**0.5)
    masked = jnp.where(allowed[None, None], scores, -1e30)
    largest = jnp.max(masked, -1, keepdims=True)
    expon = jnp.where(allowed[None, None], jnp.exp(masked - largest), 0.0)
    probs = (expon / jnp.sum(expon, -1, keepdims=True)).astype(jnp.bfloat16)
    output = jnp.einsum("kgts,skd->tkgd", probs, values_proj, preferred_element_type=jnp.float32)
    attended = output.astype(jnp.bfloat16).reshape(rows, local_heads * HEAD)
    all_heads = lax.all_gather(attended, "mp", axis=1, tiled=True)
    projected = jnp.dot(all_heads, whole_out, preferred_element_type=jnp.float32)
    feature_count = w_out.shape[1]
    own_states = lax.dynamic_slice_in_dim(
        states, lax.axis_index("mp") * feature_count, feature_count, 1
    )
    residual = own_states + projected
    square_sum, head_sum = lax.psum(
        (jnp.sum(residual * residual, 1), jnp.sum(residual * value_weight[None, :], 1)), "mp"
    )
    value = head_sum * lax.rsqrt(square_sum / width + epsilon)
    following = from_behind(old_values[:1], "dp", -1)
    next_old = jnp.concatenate([old_values[1:], following])
    booted = jnp.where(finished > 0, (1.0 - stopped) * old_values, next_old)
    delta = rewards + discount * booted - old_values
    keep_rate = discount * trace_decay
    spacing = (order[None, :] - order[:, None]).astype(jnp.float32)
    forward_mask = (spacing >= 0.0) & same_episode
    decay_matrix = jnp.where(
        forward_mask, jnp.power(jnp.float32(keep_rate), jnp.maximum(spacing, 0.0)), 0.0
    )
    local_part = jnp.dot(decay_matrix, delta, precision=lax.Precision.HIGHEST)
    remaining = (rows - order).astype(jnp.float32)
    reach = jnp.where(episode == episode[-1], jnp.power(jnp.float32(keep_rate), remaining), 0.0) * (
        1.0 - finished[-1]
    )

    def compose(earlier, later_map):
        return (later_map[0] + later_map[1] * earlier[0], later_map[1] * earlier[1])

    prefix = carried_in(
        (local_part[:1], reach[:1]),
        "dp",
        compose,
        (jnp.zeros((1,), jnp.float32), jnp.ones((1,), jnp.float32)),
    )
    incoming = prefix[0][0]
    advantage = local_part + reach * incoming
    returns = advantage + old_values
    clipped = old_values + jnp.clip(value - old_values, -clip_range, clip_range)
    terms = jnp.maximum((value - returns) ** 2, (clipped - returns) ** 2)
    total_loss = lax.psum(jnp.sum(terms), "dp")
    value_loss = 0.5 * total_loss / (rows * lax.axis_size("dp"))
    return (value, advantage, value_loss)


def solution(mesh):
    return jax.shard_map(
        body,
        mesh=mesh,
        in_specs=(
            P("dp", None),
            P("dp", "mp"),
            P("dp", "mp"),
            P("dp", "mp"),
            P("dp", "mp"),
            P("mp"),
            P("dp"),
            P("dp"),
            P(),
            P(),
        ),
        out_specs=(P("dp"), P("dp"), P()),
        check_vma=False,
    )
```

profile of v0, /device:TPU:0, one launch (start us, length us, event | category | flops | bytes accessed | tf_op | source)
XLA Modules:
  0.0 487.3 jit_solution(12846572343256018310)
XLA Ops:
  7.2 0.7 all-gather.10.cloned.1.call-update
  7.9 0.7 all-gather.8.cloned.1.call-update
  8.7 0.7 all-gather.12.cloned.1.call-update
  9.4 0.5 all-gather.16.cloned.1.call-update
  10.0 0.0 all-gather.14.cloned.1.call-start
  10.0 0.7 copy.25
  10.8 0.1 reduce-window.7
  10.9 0.1 reduce
  11.0 0.8 fusion.22
  11.8 3.1 multiply_reduce_fusion
  14.9 0.2 compare_and_fusion.1
  15.1 1.0 multiply_cosine_fusion
  16.1 47.2 %all-gather.10.cloned.1.call-done = bf16[4096,512]{1,0:T(8,128)(2,1)} async-done(((bf16[256,512]{1,0:T(8,128)(2,1)}), bf16[4096,512]{1,0:T(8,128)(2,1)}) %all-gather.10.cloned.1.call-update) | async-done | bytes 4194320 | tf_op jit(solution)/shard_map/all_gather | solution.py:58
  63.3 5.9 %fusion.32 = f32[512,512]{0,1:T(8,128)S(1)} fusion(bf16[4096,512]{1,0:T(8,128)(2,1)} %all-gather.10.cloned.1.call-done, f32[512]{0:T(512)S(1)} %add_rsqrt_fusion, bf16[512,4096]{1,0:T(8,128)(2,1)} %param.12), kind=kOutput, calls=%fused_computation.70 | convolution fusion | flops 2153775104 | bytes 9439232 | tf_op jit(solution)/shard_map/dot_general | solution.py:64
  69.2 0.1 fusion.33
  69.3 0.3 copy.34
  69.6 0.3 copy.35
  69.9 1.1 subtract_convert_fusion.1
  71.0 43.3 %all-gather.8.cloned.1.call-done = bf16[4096,512]{1,0:T(8,128)(2,1)} async-done(((bf16[256,512]{1,0:T(8,128)(2,1)}), bf16[4096,512]{1,0:T(8,128)(2,1)}) %all-gather.8.cloned.1.call-update) | async-done | bytes 4194320 | tf_op jit(solution)/shard_map/all_gather | solution.py:59
  114.4 5.9 %convolution_convert_fusion = bf16[512,512]{0,1:T(8,128)(2,1)S(1)} fusion(bf16[4096,512]{1,0:T(8,128)(2,1)} %all-gather.8.cloned.1.call-done, f32[512]{0:T(512)S(1)} %add_rsqrt_fusion, bf16[512,4096]{1,0:T(8,128)(2,1)} %param.12), kind=kOutput, calls=%fused_computation.26 | convolution fusion | flops 2154037248 | bytes 8914944 | tf_op jit(solution)/shard_map/dot_general | solution.py:64
  120.3 121.2 %all-gather.12.cloned.1.call-done = bf16[4096,2048]{1,0:T(8,128)(2,1)} async-done(((bf16[256,2048]{1,0:T(8,128)(2,1)}), bf16[4096,2048]{1,0:T(8,128)(2,1)}) %all-gather.12.cloned.1.call-update) | async-done | bytes 16777232 | tf_op jit(solution)/shard_map/all_gather | solution.py:57
  241.5 13.2 %convolution_bitcast_fusion = f32[64,8,16,128]{3,1,2,0:T(8,128)S(1)} fusion(bf16[4096,2048]{1,0:T(8,128)(2,1)} %all-gather.12.cloned.1.call-done, f32[512]{0:T(512)S(1)} %add_rsqrt_fusion, bf16[512,4096]{1,0:T(8,128)(2,1)} %param.12), kind=kOutput, calls=%fused_computation.18 | convolution fusion | flops 8596226048 | bytes 25167872 | tf_op jit(solution)/shard_map/dot_general | solution.py:64
  254.8 0.9 copy.36
  255.7 1.8 subtract_convert_fusion
  257.5 0.5 copy.29
  258.1 0.5 copy.28
  258.6 8.1 %fusion.6 = f32[4,512,512,4]{2,1,3,0:T(8,128)} fusion(bf16[512,4,4,64]{3,0,2,1:T(8,128)(2,1)S(1)} %bitcast.53, bf16[512,4,4,64]{3,0,2,1:T(8,128)(2,1)S(1)} %bitcast.54, bf16[512,4,64]{2,0,1:T(8,128)(2,1)S(1)} %copy-done, bf16[512,4,64]{2,0,1:T(8,128)(2,1)S(1)} %get-tuple-element.113), kind=kOutput, calls=%fused_computation.19 | convolution fusion | flops 1078984704 | bytes 19398656 | tf_op jit(solution)/shard_map/tkgd,skd->kgts/dot_general | solution.py:84
  266.8 17.9 %fusion.34 = (f32[4,4,512]{2,1,0:T(4,128)S(1)}, f32[4,4,512,512]{2,3,1,0:T(8,128)}) fusion(f32[4,512,512,4]{2,1,3,0:T(8,128)} %fusion.6, pred[512,512]{0,1:T(8,128)(4,1)S(1)} %compare_and_fusion.1), kind=kOutput, calls=%fused_computation.72 | output fusion | flops 29360640 | bytes 33849344 | tf_op jit(solution)/shard_map/sub | solution.py:92
  284.7 8.6 %fusion.10 = bf16[4,128,4,512]{3,1,2,0:T(8,128)(2,1)} fusion(bf16[512,4,128,1]{0,2,3,1:T(8,128)(2,1)S(1)} %bitcast.63, f32[4,4,512,512]{2,3,1,0:T(8,128)} %get-tuple-element.120, f32[4,4,512]{2,1,0:T(4,128)S(1)} %get-tuple-element.119), kind=kOutput, calls=%fused_computation.23 | convolution fusion | flops 1083179008 | bytes 19431424 | tf_op jit(solution)/shard_map/kgts,skd->tkgd/dot_general | solution.py:94
  293.4 0.5 slice.35
  293.9 1.3 collective-permute-start
  295.2 6.5 %convert_element_type.45 = f32[512,4096]{1,0:T(8,128)} convert(bf16[512,4096]{1,0:T(8,128)(2,1)} %param.12) | non-fusion elementwise | flops 2097152 | bytes 12582912 | tf_op jit(solution)/shard_map/convert_element_type | solution.py:52
  301.7 0.6 slice.36
  302.4 0.1 slice.34
  302.4 0.1 compare_reduce_fusion
  302.5 0.6 slice.37
  303.8 0.6 dynamic-slice
  304.4 0.7 select_multiply_fusion
  305.1 0.7 slice_dynamic-update-slice_fusion
  305.8 0.7 fusion.25
  306.5 1.1 fusion.11
  307.6 0.7 slice_dynamic-update-slice_fusion.1
  308.3 34.8 %all-reduce.2 = (f32[16]{0:T(128)S(1)}, f32[16]{0:T(128)S(1)}) all-reduce(f32[16]{0:T(128)S(1)} %slice_dynamic-update-slice_fusion.1, f32[16]{0:T(128)S(1)} %slice_dynamic-update-slice_fusion), channel_id=2, replica_groups=mesh['dp'=16,'mp'=2] {'dp'}, use_global_device_ids=true, to_apply=%add | all-reduce | flops 32 | bytes 256
  343.1 28.6 %while.14 = (s32[]{:T(128)}, f32[1]{0:T(128)}, s32[]{:T(128)}, f32[16,1]{0,1:T(1,128)S(1)}, f32[16,1]{0,1:T(1,128)S(1)}, /*index=5*/s32[]{:T(128)}, s32[]{:T(128)}, s32[]{:T(128)}, s32[]{:T(128)}) while((s32[]{:T(128)}, f32[1]{0:T(128)}, s32[]{:T(128)}, f32[16,1]{0,1:T(1,128)S(1)}, f32[16,1]{0,1:T(1,128)S(1)}, /*index=5*/s32[]{:T(128)}, ...), condition=%wide.region_12.13_spmd, body=%wide.region_11.12_spmd.sunk | while | flops 8 | bytes 183 | solution.py:33
  343.1 0.6 constant_dynamic-slice_fusion.3
  345.0 0.6 constant_dynamic-slice_fusion.3
  346.9 0.6 constant_dynamic-slice_fusion.3
  348.9 0.6 constant_dynamic-slice_fusion.3
  350.8 0.6 constant_dynamic-slice_fusion.3
  352.7 0.6 constant_dynamic-slice_fusion.3
  354.6 0.6 constant_dynamic-slice_fusion.3
  356.5 0.6 constant_dynamic-slice_fusion.3
  358.4 0.6 constant_dynamic-slice_fusion.3
  360.3 0.6 constant_dynamic-slice_fusion.3
  362.2 0.6 constant_dynamic-slice_fusion.3
  364.1 0.6 constant_dynamic-slice_fusion.3
  366.0 0.6 constant_dynamic-slice_fusion.3
  367.9 0.6 constant_dynamic-slice_fusion.3
  369.8 0.6 constant_dynamic-slice_fusion.3
  371.7 53.4 %all-gather.14.cloned.1.call-done = bf16[512,4096]{0,1:T(8,128)(2,1)} async-done(((bf16[512,2048]{0,1:T(8,128)(2,1)}), bf16[512,4096]{0,1:T(8,128)(2,1)}) %all-gather.14.cloned.1.call-update) | async-done | bytes 4194320 | tf_op jit(solution)/shard_map/all_gather | solution.py:96
  425.1 14.6 %multiply_reduce_fusion.1 = (f32[512]{0:T(512)S(1)}, f32[512]{0:T(512)S(1)}) fusion(f32[2048]{0:T(1024)S(1)} %copy-done.3, bf16[512,4096]{0,1:T(8,128)(2,1)} %all-gather.14.cloned.1.call-done, bf16[4096,2048]{1,0:T(8,128)(2,1)} %all-gather.16.cloned.1.call-done, f32[512,4096]{1,0:T(8,128)} %convert_element_type.45, s32[]{:T(128)S(6)} %select_n.35), kind=kOutput, calls=%fused_computation.13 | convolution fusion | flops 8595177472 | bytes 25178116 | tf_op jit(solution)/shard_map/dot_general | solution.py:97
  439.7 4.9 %all-reduce.3 = (f32[512]{0:T(512)S(1)}, f32[512]{0:T(512)S(1)}) all-reduce(f32[512]{0:T(512)S(1)} %get-tuple-element.89, f32[512]{0:T(512)S(1)} %get-tuple-element.88), channel_id=1, replica_groups=mesh['dp'=16,'mp'=2] {'mp'}, use_global_device_ids=true, to_apply=%region_6.7 | all-reduce | flops 1024 | bytes 8192 | tf_op jit(solution)/shard_map/psum | solution.py:103
  444.7 1.9 maximum_reduce_fusion
  446.5 32.5 %psum.23 = f32[]{:T(128)} all-reduce(f32[]{:T(128)} %get-tuple-element.106), channel_id=1, replica_groups=mesh['dp'=16,'mp'=2] {'dp'}, use_global_device_ids=true, to_apply=%region_14.15 | all-reduce | flops 1 | bytes 8 | tf_op jit(solution)/shard_map/psum | solution.py:137
  (25 shorter events, 0.3 us)
Async XLA Ops:
  7.2 56.1 %all-gather.10.cloned.1.call-start = ((), (), s32[]{:S(2)}) async-start(), calls=%async_computation.1 | async-start | bytes 4456448 | tf_op jit(solution)/shard_map/all_gather | solution.py:58
  7.9 106.5 %all-gather.8.cloned.1.call-start = ((), (), s32[]{:S(2)}) async-start(), calls=%async_computation | async-start | bytes 4456448 | tf_op jit(solution)/shard_map/all_gather | solution.py:59
  8.7 232.9 %all-gather.12.cloned.1.call-start = ((), (), s32[]{:S(2)}) async-start(), calls=%async_computation.2 | async-start | bytes 17825792 | tf_op jit(solution)/shard_map/all_gather | solution.py:57
  9.4 362.3 %all-gather.16.cloned.1.call-start = ((), (), s32[]{:S(2)}) async-start(), calls=%async_computation.4 | async-start | bytes 17825792 | tf_op jit(solution)/shard_map/all_gather | solution.py:60
  10.0 415.2 %all-gather.14.cloned.1.call-start = ((), (), s32[]{:S(2)}) async-start(), calls=%async_computation.3 | async-start | bytes 6291456 | tf_op jit(solution)/shard_map/all_gather | solution.py:96
  257.5 1.1 copy-start
  284.7 8.6 %copy-start.1 = (f32[512]{0:T(512)S(1)}, f32[512]{0:T(512)}, u32[]{:S(2)}) copy-start(f32[512]{0:T(512)} %param.19) | copy-start | bytes 6148
  293.9 12.0 %collective-permute-start = (f32[1]{0:T(128)}, f32[1]{0:T(128)}, u32[]{:S(2)}, u32[]{:S(2)}) collective-permute-start(f32[1]{0:T(128)} %slice.35), channel_id=1, source_target_pairs={{2,0},{4,2},{6,4},{8,6},{10,8},{12,10},{14,12},{16,14},{18,16},{20... | collective-permute-start | bytes 20 | tf_op jit(solution)/shard_map/ppermute | solution.py:17
  295.2 8.6 %copy-start.4 = (u32[32]{0:T(128)S(1)}, u32[32]{0:T(128)}, u32[]{:S(2)}) copy-start(u32[32]{0:T(128)} %constant.106) | copy-start | bytes 388
  295.2 10.7 %copy-start.2 = (f32[512]{0:T(512)S(1)}, f32[512]{0:T(512)}, u32[]{:S(2)}) copy-start(f32[512]{0:T(512)} %param.18) | copy-start | bytes 6148
  295.2 130.0 %copy-start.3 = (f32[2048]{0:T(1024)S(1)}, f32[2048]{0:T(1024)}, u32[]{:S(2)}) copy-start(f32[2048]{0:T(1024)} %param.17) | copy-start | bytes 24580
Sparse Core Ops, SparseCore 0:
  10.1 53.0 all-gather.9
  65.4 48.8 all-gather.7
  116.5 124.9 all-gather.11
  243.6 125.2 all-gather.15
  370.2 54.8 all-gather.13
where the time goes:
time: 488 us; the launch traced here: 487 us
  waiting for transfers between devices  268 us (55%)
  blocking collectives  72.2 us (15%)
  matrix products  57.5 us (12%)
  other arithmetic  36 us (7%)
  loops' own time  19.3 us (4%)
  local copies, waits for them, and re-layouts  16.7 us (3%)
  between operations  16.4 us (3%)
    all_gather x1, waiting for transfers between devices, body(): lax.all_gather(w_query, 'dp', axis=0, tiled=True)  121 us
    all_gather x1, waiting for transfers between devices, body(): all_heads = lax.all_gather(attended, 'mp', axis=1, tiled=True)  53.4 us
    all_gather x1, waiting for transfers between devices, body(): lax.all_gather(w_key, 'dp', axis=0, tiled=True)  47.2 us
    all_gather x1, waiting for transfers between devices, body(): lax.all_gather(w_value, 'dp', axis=0, tiled=True)  43.3 us
    unnamed x1, blocking collectives  34.8 us
    psum x1, blocking collectives, body(): total_loss = lax.psum(jnp.sum(terms), 'dp')  32.5 us
    dot_general x3, matrix products, body(): jnp.dot(normed, piece, preferred_element_type=jnp.float32)  25 us
    another operation x1, loops' own time, carried_in(): return lax.fori_loop(0, ahead, one, state)  19.3 us
  transfers between devices with their start and end apart: 6, of which 4 were waited for; matrix products, arithmetic and copies ran while one was open for 19% of the time, Pallas kernels for 0%

commit v1 on v0

--- a/solution.py
+++ b/solution.py
@@ -1,3 +1,4 @@
+import functools
 import jax
 import jax.numpy as jnp
 from jax import lax
@@ -9,6 +10,36 @@
 clip_range = 0.2
 epsilon = 1e-05
 rope_base = 500000.0
+
+
+def detail_scenes_over_axis(base_x, ax_name):
+    formed = jax.lax.axis_index(ax_name)
+    h_now = jax.lax.axis_size(ax_name)
+    o_now, new, step_out = (h_now, formed, base_x.shape[0])
+    by_rank = [j * o_now if u == 0 else j for u, j in enumerate(base_x.shape)]
+    long_array = jnp.zeros(by_rank, base_x.dtype)
+    before = everything = base_x
+    arr_next = lax.dynamic_update_slice_in_dim(long_array, base_x, new * step_out, axis=0)
+    for hop_no in range(1, o_now // 2 + 1):
+        y2 = range(o_now)
+        field_out = map(lambda u: (u, (u + 1) % o_now), y2)
+        block_next = list(field_out)
+        before = jax.lax.ppermute(before, ax_name, block_next)
+        arr_next = lax.dynamic_update_slice_in_dim(
+            arr_next, before, (new - hop_no) % o_now * step_out, axis=0
+        )
+        if 2 * hop_no < o_now:
+            even = range(o_now)
+            r2 = map(lambda u: (u, (u - 1) % o_now), even)
+            n_now = list(r2)
+            everything = jax.lax.ppermute(everything, ax_name, n_now)
+            arr_next = lax.dynamic_update_slice_in_dim(
+                arr_next, everything, (new + hop_no) % o_now * step_out, axis=0
+            )
+    return arr_next
+
+
+watch_stacks_all_over_axis = functools.partial(detail_scenes_over_axis, ax_name="dp")
 
 
 def from_behind(array, axis, by):
@@ -56,7 +87,7 @@
     pieces = (
         lax.all_gather(w_query, "dp", axis=0, tiled=True),
         lax.all_gather(w_key, "dp", axis=0, tiled=True),
-        lax.all_gather(w_value, "dp", axis=0, tiled=True),
+        watch_stacks_all_over_axis(w_value),
         lax.all_gather(w_out, "dp", axis=0, tiled=True),
     )
     add_pieces = pieces[:3]

time: 488 us -> 454 us (0.930)
  waiting for transfers between devices: 268 us -> 189 us
  starting transfers between devices: 1.47 us -> 35.3 us
  local copies, waits for them, and re-layouts: 16.7 us -> 29.4 us
    all_gather x1, waiting for transfers between devices: 47.2 us -> 0.01 us  [body(): lax.all_gather(w_key, 'dp', axis=0, tiled=True)]
    all_gather x1 -> x0, waiting for transfers between devices: 43.3 us -> none  [body(): lax.all_gather(w_value, 'dp', axis=0, tiled=True)]
    ppermute x0 -> x15, starting transfers between devices: none -> 33.9 us  [the longest x7 32.2 us: detail_scenes_over_axis(): everything = jax.lax.ppermute(everything, ax_name, n_now)]
    ppermute x0 -> x15, waiting for transfers between devices: none -> 26.9 us  [the longest x8 21.8 us: detail_scenes_over_axis(): before = jax.lax.ppermute(before, ax_name, block_next)]
    all_gather x1, waiting for transfers between devices: 121 us -> 104 us  [body(): lax.all_gather(w_query, 'dp', axis=0, tiled=True)]
    dynamic_update_slice x0 -> x16, local copies, waits for them, and re-layouts: none -> 11.5 us  [the longest x8 5.76 us: detail_scenes_over_axis(): lax.dynamic_update_slice_in_dim(arr_next, before, (new - hop_no) % o_now...]
  transfers between devices with their start and end apart: 6 -> 20, of which waited for: 4 -> 11; matrix products, arithmetic and copies ran while one was open for 19% -> 23% of each run, Pallas kernels for 0% -> 0%
where the time goes in v1:
time: 454 us; the launch traced here: 453 us
  waiting for transfers between devices  189 us (42%)
  blocking collectives  72.1 us (16%)
  matrix products  57.5 us (13%)
  starting transfers between devices  35.3 us (8%)
  other arithmetic  35 us (8%)
  local copies, waits for them, and re-layouts  29.4 us (6%)
  loops' own time  18.3 us (4%)
  between operations  16.5 us (4%)
    all_gather x1, waiting for transfers between devices, body(): lax.all_gather(w_query, 'dp', axis=0, tiled=True)  104 us
    all_gather x1, waiting for transfers between devices, body(): all_heads = lax.all_gather(attended, 'mp', axis=1, tiled=True)  55.4 us
    unnamed x1, blocking collectives  34.7 us
    psum x1, blocking collectives, body(): total_loss = lax.psum(jnp.sum(terms), 'dp')  32.5 us
    ppermute x7, starting transfers between devices, detail_scenes_over_axis(): everything = jax.lax.ppermute(everything, ax_name, n_now)  32.2 us
    dot_general x3, matrix products, body(): jnp.dot(normed, piece, preferred_element_type=jnp.float32)  25.1 us
    ppermute x8, waiting for transfers between devices, detail_scenes_over_axis(): before = jax.lax.ppermute(before, ax_name, block_next)  21.8 us
    another operation x1, loops' own time, carried_in(): return lax.fori_loop(0, ahead, one, state)  18.3 us
  transfers between devices with their start and end apart: 20, of which 11 were waited for; matrix products, arithmetic and copies ran while one was open for 23% of the time, Pallas kernels for 0%

profile of v1, /device:TPU:0, one launch (start us, length us, event | category | flops | bytes accessed | tf_op | source)
XLA Modules:
  0.0 453.0 jit_solution(18310665345968425301)
XLA Ops:
  7.2 0.7 all-gather.7.cloned.1.call-update
  8.0 0.7 all-gather.9.cloned.1.call-update
  8.7 0.7 all-gather.13.cloned.1.call-update
  10.0 5.0 %collective-permute-start.1 = (bf16[256,512]{1,0:T(8,128)(2,1)}, bf16[256,512]{1,0:T(8,128)(2,1)S(1)}, u32[]{:S(2)}, u32[]{:S(2)}) collective-permute-start(bf16[256,512]{1,0:T(8,128)(2,1)} %param.15), channel_id=1, source_target_pairs={{0,30},{2,0},{4,2},{6,4},{8,6},{10,8},{12,10},{14,12},{16,14},{18,... | collective-permute-start | bytes 786440 | tf_op jit(solution)/shard_map/ppermute | solution.py:35
  15.1 3.1 multiply_reduce_fusion
  18.5 1.0 multiply_cosine_fusion
  19.6 4.5 collective-permute-start.3
  24.2 6.9 %collective-permute-done.2 = bf16[256,512]{1,0:T(8,128)(2,1)S(1)} collective-permute-done((bf16[256,512]{1,0:T(8,128)(2,1)S(1)}, bf16[256,512]{1,0:T(8,128)(2,1)S(1)}, u32[]{:S(2)}, u32[]{:S(2)}) %collective-permute-start.2) | collective-permute-done | bytes 262176 | tf_op jit(solution)/shard_map/ppermute | solution.py:27
  31.4 4.5 collective-permute-start.5
  35.8 3.9 collective-permute-done.4
  39.8 2.2 broadcast_in_dim.30
  42.0 0.7 constant_dynamic-update-slice_fusion.15
  42.8 0.7 constant_dynamic-update-slice_fusion.14
  43.5 4.4 collective-permute-start.7
  47.9 0.7 constant_dynamic-update-slice_fusion.13
  48.6 1.9 collective-permute-done.6
  50.6 0.7 constant_dynamic-update-slice_fusion.12
  51.3 0.7 constant_dynamic-update-slice_fusion.11
  52.1 4.7 %collective-permute-start.9 = (bf16[256,512]{1,0:T(8,128)(2,1)S(1)}, bf16[256,512]{1,0:T(8,128)(2,1)S(1)}, u32[]{:S(2)}, u32[]{:S(2)}) collective-permute-start(bf16[256,512]{1,0:T(8,128)(2,1)S(1)} %collective-permute-done.7), channel_id=1, source_target_pairs={{0,30},{2,0},{4,2},{6,4},{8,6},{10,8},{12,10},{14,12},{16,14},{18,... | collective-permute-start | bytes 786440 | tf_op jit(solution)/shard_map/ppermute | solution.py:35
  56.8 0.7 constant_dynamic-update-slice_fusion.10
  57.5 2.3 collective-permute-done.8
  59.8 0.7 constant_dynamic-update-slice_fusion.9
  60.5 0.7 constant_dynamic-update-slice_fusion.8
  61.2 4.4 collective-permute-start.11
  65.7 0.7 constant_dynamic-update-slice_fusion.7
  66.4 2.0 collective-permute-done.10
  68.4 1.1 collective-permute-start.12
  69.5 0.7 constant_dynamic-update-slice_fusion.6
  70.2 0.7 constant_dynamic-update-slice_fusion.5
  71.0 3.3 collective-permute-done.11
  74.3 4.6 %collective-permute-start.13 = (bf16[256,512]{1,0:T(8,128)(2,1)S(1)}, bf16[256,512]{1,0:T(8,128)(2,1)S(1)}, u32[]{:S(2)}, u32[]{:S(2)}) collective-permute-start(bf16[256,512]{1,0:T(8,128)(2,1)S(1)} %collective-permute-done.11), channel_id=1, source_target_pairs={{0,30},{2,0},{4,2},{6,4},{8,6},{10,8},{12,10},{14,12},{16,14},{18,... | collective-permute-start | bytes 786440 | tf_op jit(solution)/shard_map/ppermute | solution.py:35
  78.9 0.7 constant_dynamic-update-slice_fusion.4
  79.6 0.7 constant_dynamic-update-slice_fusion.3
  80.3 0.7 constant_dynamic-update-slice_fusion.2
  81.1 1.7 collective-permute-done.13
  82.8 0.7 constant_dynamic-update-slice_fusion.1
  83.5 4.6 %collective-permute-done.14 = bf16[256,512]{1,0:T(8,128)(2,1)S(1)} collective-permute-done((bf16[256,512]{1,0:T(8,128)(2,1)S(1)}, bf16[256,512]{1,0:T(8,128)(2,1)S(1)}, u32[]{:S(2)}, u32[]{:S(2)}) %collective-permute-start.14) | collective-permute-done | bytes 262176 | tf_op jit(solution)/shard_map/ppermute | solution.py:27
  88.1 0.7 constant_dynamic-update-slice_fusion
  88.9 5.9 %convolution_convert_fusion = bf16[512,512]{0,1:T(8,128)(2,1)} fusion(bf16[4096,512]{1,0:T(8,128)(2,1)} %constant_dynamic-update-slice_fusion, f32[512]{0:T(512)S(1)} %add_rsqrt_fusion, bf16[512,4096]{1,0:T(8,128)(2,1)S(1)} %copy-done), kind=kOutput, calls=%fused_computation.26 | convolution fusion | flops 2154037248 | bytes 8914944 | tf_op jit(solution)/shard_map/dot_general | solution.py:95
  94.8 5.9 %fusion.32 = f32[512,512]{0,1:T(8,128)S(1)} fusion(bf16[4096,512]{1,0:T(8,128)(2,1)} %all-gather.7.cloned.1.call-done, f32[512]{0:T(512)S(1)} %add_rsqrt_fusion, bf16[512,4096]{1,0:T(8,128)(2,1)} %param.12), kind=kOutput, calls=%fused_computation.86 | convolution fusion | flops 2153775104 | bytes 9439232 | tf_op jit(solution)/shard_map/dot_general | solution.py:95
  101.5 1.1 subtract_convert_fusion.1
  102.6 104.5 %all-gather.9.cloned.1.call-done = bf16[4096,2048]{1,0:T(8,128)(2,1)} async-done(((bf16[256,2048]{1,0:T(8,128)(2,1)}), bf16[4096,2048]{1,0:T(8,128)(2,1)}) %all-gather.9.cloned.1.call-update) | async-done | bytes 16777232 | tf_op jit(solution)/shard_map/all_gather | solution.py:88
  207.1 13.2 %convolution_bitcast_fusion = f32[64,8,16,128]{3,1,2,0:T(8,128)S(1)} fusion(bf16[4096,2048]{1,0:T(8,128)(2,1)} %all-gather.9.cloned.1.call-done, f32[512]{0:T(512)S(1)} %add_rsqrt_fusion, bf16[512,4096]{1,0:T(8,128)(2,1)} %param.12), kind=kOutput, calls=%fused_computation.18 | convolution fusion | flops 8596226048 | bytes 25167872 | tf_op jit(solution)/shard_map/dot_general | solution.py:95
  220.3 0.9 copy.36
  221.2 1.6 subtract_convert_fusion
  223.9 8.2 %fusion.6 = f32[4,512,512,4]{2,1,3,0:T(8,128)} fusion(bf16[512,4,4,64]{3,0,2,1:T(8,128)(2,1)S(1)} %bitcast.53, bf16[512,4,4,64]{3,0,2,1:T(8,128)(2,1)S(1)} %bitcast.54, bf16[512,4,64]{2,0,1:T(8,128)(2,1)S(1)} %copy-done.1, bf16[512,4,64]{2,0,1:T(8,128)(2,1)S(1)} %get-tuple-element.113), kind=kOutput, calls=%fused_computation.19 | convolution fusion | flops 1078984704 | bytes 19398656 | tf_op jit(solution)/shard_map/tkgd,skd->kgts/dot_general | solution.py:115
  232.1 18.0 %fusion.34 = (f32[4,4,512]{2,1,0:T(4,128)S(1)}, f32[4,4,512,512]{2,3,1,0:T(8,128)}) fusion(f32[4,512,512,4]{2,1,3,0:T(8,128)} %fusion.6, pred[512,512]{0,1:T(8,128)(4,1)S(1)} %compare_and_fusion.1), kind=kOutput, calls=%fused_computation.88 | output fusion | flops 29360640 | bytes 33849344 | tf_op jit(solution)/shard_map/sub | solution.py:123
  250.1 8.6 %fusion.10 = bf16[4,128,4,512]{3,1,2,0:T(8,128)(2,1)} fusion(bf16[512,4,128,1]{0,2,3,1:T(8,128)(2,1)S(1)} %bitcast.63, f32[4,4,512,512]{2,3,1,0:T(8,128)} %get-tuple-element.120, f32[4,4,512]{2,1,0:T(4,128)S(1)} %get-tuple-element.119), kind=kOutput, calls=%fused_computation.23 | convolution fusion | flops 1083179008 | bytes 19431424 | tf_op jit(solution)/shard_map/kgts,skd->tkgd/dot_general | solution.py:125
  259.2 1.3 collective-permute-start.15
  261.2 6.5 %convert_element_type.45 = f32[512,4096]{1,0:T(8,128)} convert(bf16[512,4096]{1,0:T(8,128)(2,1)} %param.12) | non-fusion elementwise | flops 2097152 | bytes 12582912 | tf_op jit(solution)/shard_map/convert_element_type | solution.py:83
  267.8 0.7 slice.37
  268.5 0.6 dynamic-slice
  269.8 0.6 select_multiply_fusion
  270.4 0.7 slice_dynamic-update-slice_fusion
  271.1 0.6 fusion.25
  271.8 1.1 fusion.11
  272.9 0.7 slice_dynamic-update-slice_fusion.1
  273.6 34.7 %all-reduce.2 = (f32[16]{0:T(128)S(1)}, f32[16]{0:T(128)S(1)}) all-reduce(f32[16]{0:T(128)S(1)} %slice_dynamic-update-slice_fusion.1, f32[16]{0:T(128)S(1)} %slice_dynamic-update-slice_fusion), channel_id=2, replica_groups=mesh['dp'=16,'mp'=2] {'dp'}, use_global_device_ids=true, to_apply=%add | all-reduce | flops 32 | bytes 256
  308.3 27.1 %while.14 = (s32[]{:T(128)}, f32[1]{0:T(128)}, s32[]{:T(128)}, f32[16,1]{0,1:T(1,128)S(1)}, f32[16,1]{0,1:T(1,128)S(1)}, /*index=5*/s32[]{:T(128)}, s32[]{:T(128)}, s32[]{:T(128)}, s32[]{:T(128)}) while((s32[]{:T(128)}, f32[1]{0:T(128)}, s32[]{:T(128)}, f32[16,1]{0,1:T(1,128)S(1)}, f32[16,1]{0,1:T(1,128)S(1)}, /*index=5*/s32[]{:T(128)}, ...), condition=%wide.region_12.13_spmd, body=%wide.region_11.12_spmd.sunk | while | flops 8 | bytes 191 | solution.py:64
  335.4 55.4 %all-gather.11.cloned.1.call-done = bf16[512,4096]{0,1:T(8,128)(2,1)} async-done(((bf16[512,2048]{0,1:T(8,128)(2,1)}), bf16[512,4096]{0,1:T(8,128)(2,1)}) %all-gather.11.cloned.1.call-update) | async-done | bytes 4194320 | tf_op jit(solution)/shard_map/all_gather | solution.py:127
  390.9 14.6 %multiply_reduce_fusion.1 = (f32[512]{0:T(512)S(1)}, f32[512]{0:T(512)S(1)}) fusion(f32[2048]{0:T(1024)S(1)} %copy-done.7, bf16[512,4096]{0,1:T(8,128)(2,1)} %all-gather.11.cloned.1.call-done, bf16[4096,2048]{1,0:T(8,128)(2,1)} %all-gather.13.cloned.1.call-done, f32[512,4096]{1,0:T(8,128)} %convert_element_type.45, s32[]{:T(128)S(6)} %select_n.146), kind=kOutput, calls=%fused_computation.13 | convolution fusion | flops 8595177472 | bytes 25178116 | tf_op jit(solution)/shard_map/dot_general | solution.py:128
  405.5 4.9 %all-reduce.3 = (f32[512]{0:T(512)S(1)}, f32[512]{0:T(512)S(1)}) all-reduce(f32[512]{0:T(512)S(1)} %get-tuple-element.89, f32[512]{0:T(512)S(1)} %get-tuple-element.88), channel_id=1, replica_groups=mesh['dp'=16,'mp'=2] {'mp'}, use_global_device_ids=true, to_apply=%region_6.7 | all-reduce | flops 1024 | bytes 8192 | tf_op jit(solution)/shard_map/psum | solution.py:134
  410.4 1.8 maximum_reduce_fusion
  412.2 32.5 %psum.23 = f32[]{:T(128)} all-reduce(f32[]{:T(128)} %get-tuple-element.106), channel_id=1, replica_groups=mesh['dp'=16,'mp'=2] {'dp'}, use_global_device_ids=true, to_apply=%region_14.15 | all-reduce | flops 1 | bytes 8 | tf_op jit(solution)/shard_map/psum | solution.py:168
  (79 shorter events, 13.5 us)
Async XLA Ops:
  7.2 11.0 %copy-start.5 = (s32[64]{0:T(128)S(1)}, s32[64]{0:T(128)}, u32[]{:S(2)}) copy-start(s32[64]{0:T(128)} %param.20) | copy-start | bytes 772
  7.2 16.9 %copy-start.6 = (s32[64]{0:T(128)S(1)}, s32[64]{0:T(128)}, u32[]{:S(2)}) copy-start(s32[64]{0:T(128)} %param.21) | copy-start | bytes 772
  7.2 87.6 %all-gather.7.cloned.1.call-start = ((), (), s32[]{:S(2)}) async-start(), calls=%async_computation | async-start | bytes 4456448 | tf_op jit(solution)/shard_map/all_gather | solution.py:89
  7.9 199.2 %all-gather.9.cloned.1.call-start = ((), (), s32[]{:S(2)}) async-start(), calls=%async_computation.1 | async-start | bytes 17825792 | tf_op jit(solution)/shard_map/all_gather | solution.py:88
  8.7 326.8 %all-gather.13.cloned.1.call-start = ((), (), s32[]{:S(2)}) async-start(), calls=%async_computation.3 | async-start | bytes 17825792 | tf_op jit(solution)/shard_map/all_gather | solution.py:91
  9.4 381.5 %all-gather.11.cloned.1.call-start = ((), (), s32[]{:S(2)}) async-start(), calls=%async_computation.2 | async-start | bytes 6291456 | tf_op jit(solution)/shard_map/all_gather | solution.py:127
  9.5 10.0 %collective-permute-start = (bf16[256,512]{1,0:T(8,128)(2,1)}, bf16[256,512]{1,0:T(8,128)(2,1)S(1)}, u32[]{:S(2)}, u32[]{:S(2)}) collective-permute-start(bf16[256,512]{1,0:T(8,128)(2,1)} %param.15), channel_id=1, source_target_pairs={{0,2},{2,4},{4,6},{6,8},{8,10},{10,12},{12,14},{14,16},{16,18},{18... | collective-permute-start | bytes 786440 | tf_op jit(solution)/shard_map/ppermute | solution.py:27
  10.0 9.6 %collective-permute-start.1 = (bf16[256,512]{1,0:T(8,128)(2,1)}, bf16[256,512]{1,0:T(8,128)(2,1)S(1)}, u32[]{:S(2)}, u32[]{:S(2)}) collective-permute-start(bf16[256,512]{1,0:T(8,128)(2,1)} %param.15), channel_id=1, source_target_pairs={{0,30},{2,0},{4,2},{6,4},{8,6},{10,8},{12,10},{14,12},{16,14},{18,... | collective-permute-start | bytes 786440 | tf_op jit(solution)/shard_map/ppermute | solution.py:35
  15.1 27.0 %copy-start.2 = (bf16[256,512]{1,0:T(8,128)(2,1)S(1)}, bf16[256,512]{1,0:T(8,128)(2,1)}, u32[]{:S(2)}) copy-start(bf16[256,512]{1,0:T(8,128)(2,1)} %param.15) | copy-start | bytes 786436
  19.5 11.6 %collective-permute-start.2 = (bf16[256,512]{1,0:T(8,128)(2,1)S(1)}, bf16[256,512]{1,0:T(8,128)(2,1)S(1)}, u32[]{:S(2)}, u32[]{:S(2)}) collective-permute-start(bf16[256,512]{1,0:T(8,128)(2,1)S(1)} %collective-permute-done), channel_id=1, source_target_pairs={{0,2},{2,4},{4,6},{6,8},{8,10},{10,12},{12,14},{14,16},{16,18},{18... | collective-permute-start | bytes 786440 | tf_op jit(solution)/shard_map/ppermute | solution.py:27
  19.6 11.7 %collective-permute-start.3 = (bf16[256,512]{1,0:T(8,128)(2,1)S(1)}, bf16[256,512]{1,0:T(8,128)(2,1)S(1)}, u32[]{:S(2)}, u32[]{:S(2)}) collective-permute-start(bf16[256,512]{1,0:T(8,128)(2,1)S(1)} %collective-permute-done.1), channel_id=1, source_target_pairs={{0,30},{2,0},{4,2},{6,4},{8,6},{10,8},{12,10},{14,12},{16,14},{18,... | collective-permute-start | bytes 786440 | tf_op jit(solution)/shard_map/ppermute | solution.py:35
  31.1 8.7 %collective-permute-start.4 = (bf16[256,512]{1,0:T(8,128)(2,1)S(1)}, bf16[256,512]{1,0:T(8,128)(2,1)S(1)}, u32[]{:S(2)}, u32[]{:S(2)}) collective-permute-start(bf16[256,512]{1,0:T(8,128)(2,1)S(1)} %collective-permute-done.2), channel_id=1, source_target_pairs={{0,2},{2,4},{4,6},{6,8},{8,10},{10,12},{12,14},{14,16},{16,18},{18... | collective-permute-start | bytes 786440 | tf_op jit(solution)/shard_map/ppermute | solution.py:27
  31.4 12.1 %collective-permute-start.5 = (bf16[256,512]{1,0:T(8,128)(2,1)S(1)}, bf16[256,512]{1,0:T(8,128)(2,1)S(1)}, u32[]{:S(2)}, u32[]{:S(2)}) collective-permute-start(bf16[256,512]{1,0:T(8,128)(2,1)S(1)} %collective-permute-done.3), channel_id=1, source_target_pairs={{0,30},{2,0},{4,2},{6,4},{8,6},{10,8},{12,10},{14,12},{16,14},{18,... | collective-permute-start | bytes 786440 | tf_op jit(solution)/shard_map/ppermute | solution.py:35
  39.8 10.8 %collective-permute-start.6 = (bf16[256,512]{1,0:T(8,128)(2,1)S(1)}, bf16[256,512]{1,0:T(8,128)(2,1)S(1)}, u32[]{:S(2)}, u32[]{:S(2)}) collective-permute-start(bf16[256,512]{1,0:T(8,128)(2,1)S(1)} %collective-permute-done.4), channel_id=1, source_target_pairs={{0,2},{2,4},{4,6},{6,8},{8,10},{10,12},{12,14},{14,16},{16,18},{18... | collective-permute-start | bytes 786440 | tf_op jit(solution)/shard_map/ppermute | solution.py:27
  42.8 46.1 %copy-start = (bf16[512,4096]{1,0:T(8,128)(2,1)S(1)}, bf16[512,4096]{1,0:T(8,128)(2,1)}, u32[]{:S(2)}) copy-start(bf16[512,4096]{1,0:T(8,128)(2,1)} %param.12) | copy-start | bytes 12582916
  43.5 8.6 %collective-permute-start.7 = (bf16[256,512]{1,0:T(8,128)(2,1)S(1)}, bf16[256,512]{1,0:T(8,128)(2,1)S(1)}, u32[]{:S(2)}, u32[]{:S(2)}) collective-permute-start(bf16[256,512]{1,0:T(8,128)(2,1)S(1)} %collective-permute-done.5), channel_id=1, source_target_pairs={{0,30},{2,0},{4,2},{6,4},{8,6},{10,8},{12,10},{14,12},{16,14},{18,... | collective-permute-start | bytes 786440 | tf_op jit(solution)/shard_map/ppermute | solution.py:35
  50.6 9.2 %collective-permute-start.8 = (bf16[256,512]{1,0:T(8,128)(2,1)S(1)}, bf16[256,512]{1,0:T(8,128)(2,1)S(1)}, u32[]{:S(2)}, u32[]{:S(2)}) collective-permute-start(bf16[256,512]{1,0:T(8,128)(2,1)S(1)} %collective-permute-done.6), channel_id=1, source_target_pairs={{0,2},{2,4},{4,6},{6,8},{8,10},{10,12},{12,14},{14,16},{16,18},{18... | collective-permute-start | bytes 786440 | tf_op jit(solution)/shard_map/ppermute | solution.py:27
  52.1 9.2 %collective-permute-start.9 = (bf16[256,512]{1,0:T(8,128)(2,1)S(1)}, bf16[256,512]{1,0:T(8,128)(2,1)S(1)}, u32[]{:S(2)}, u32[]{:S(2)}) collective-permute-start(bf16[256,512]{1,0:T(8,128)(2,1)S(1)} %collective-permute-done.7), channel_id=1, source_target_pairs={{0,30},{2,0},{4,2},{6,4},{8,6},{10,8},{12,10},{14,12},{16,14},{18,... | collective-permute-start | bytes 786440 | tf_op jit(solution)/shard_map/ppermute | solution.py:35
  59.8 8.7 %collective-permute-start.10 = (bf16[256,512]{1,0:T(8,128)(2,1)S(1)}, bf16[256,512]{1,0:T(8,128)(2,1)S(1)}, u32[]{:S(2)}, u32[]{:S(2)}) collective-permute-start(bf16[256,512]{1,0:T(8,128)(2,1)S(1)} %collective-permute-done.8), channel_id=1, source_target_pairs={{0,2},{2,4},{4,6},{6,8},{8,10},{10,12},{12,14},{14,16},{16,18},{18... | collective-permute-start | bytes 786440 | tf_op jit(solution)/shard_map/ppermute | solution.py:27
  61.2 13.1 %collective-permute-start.11 = (bf16[256,512]{1,0:T(8,128)(2,1)S(1)}, bf16[256,512]{1,0:T(8,128)(2,1)S(1)}, u32[]{:S(2)}, u32[]{:S(2)}) collective-permute-start(bf16[256,512]{1,0:T(8,128)(2,1)S(1)} %collective-permute-done.9), channel_id=1, source_target_pairs={{0,30},{2,0},{4,2},{6,4},{8,6},{10,8},{12,10},{14,12},{16,14},{18,... | collective-permute-start | bytes 786440 | tf_op jit(solution)/shard_map/ppermute | solution.py:35
  68.4 11.2 %collective-permute-start.12 = (bf16[256,512]{1,0:T(8,128)(2,1)S(1)}, bf16[256,512]{1,0:T(8,128)(2,1)S(1)}, u32[]{:S(2)}, u32[]{:S(2)}) collective-permute-start(bf16[256,512]{1,0:T(8,128)(2,1)S(1)} %collective-permute-done.10), channel_id=1, source_target_pairs={{0,2},{2,4},{4,6},{6,8},{8,10},{10,12},{12,14},{14,16},{16,18},{18... | collective-permute-start | bytes 786440 | tf_op jit(solution)/shard_map/ppermute | solution.py:27
  74.3 8.5 %collective-permute-start.13 = (bf16[256,512]{1,0:T(8,128)(2,1)S(1)}, bf16[256,512]{1,0:T(8,128)(2,1)S(1)}, u32[]{:S(2)}, u32[]{:S(2)}) collective-permute-start(bf16[256,512]{1,0:T(8,128)(2,1)S(1)} %collective-permute-done.11), channel_id=1, source_target_pairs={{0,30},{2,0},{4,2},{6,4},{8,6},{10,8},{12,10},{14,12},{16,14},{18,... | collective-permute-start | bytes 786440 | tf_op jit(solution)/shard_map/ppermute | solution.py:35
  79.6 8.5 %collective-permute-start.14 = (bf16[256,512]{1,0:T(8,128)(2,1)S(1)}, bf16[256,512]{1,0:T(8,128)(2,1)S(1)}, u32[]{:S(2)}, u32[]{:S(2)}) collective-permute-start(bf16[256,512]{1,0:T(8,128)(2,1)S(1)} %collective-permute-done.12), channel_id=1, source_target_pairs={{0,2},{2,4},{4,6},{6,8},{8,10},{10,12},{12,14},{14,16},{16,18},{18... | collective-permute-start | bytes 786440 | tf_op jit(solution)/shard_map/ppermute | solution.py:27
  222.8 1.1 copy-start.1
  232.1 18.0 %copy-start.8 = (bf16[512,512]{0,1:T(8,128)(2,1)S(1)}, bf16[512,512]{0,1:T(8,128)(2,1)}, u32[]{:S(2)}) copy-start(bf16[512,512]{0,1:T(8,128)(2,1)} %convolution_convert_fusion) | copy-start | bytes 1572868
  250.1 8.6 %copy-start.3 = (f32[512]{0:T(512)S(1)}, f32[512]{0:T(512)}, u32[]{:S(2)}) copy-start(f32[512]{0:T(512)} %param.19) | copy-start | bytes 6148
  259.2 11.9 %collective-permute-start.15 = (f32[1]{0:T(128)}, f32[1]{0:T(128)}, u32[]{:S(2)}, u32[]{:S(2)}) collective-permute-start(f32[1]{0:T(128)} %slice.35), channel_id=1, source_target_pairs={{2,0},{4,2},{6,4},{8,6},{10,8},{12,10},{14,12},{16,14},{18,16},{20... | collective-permute-start | bytes 20 | tf_op jit(solution)/shard_map/ppermute | solution.py:48
  261.2 7.3 %copy-start.9 = (u32[32]{0:T(128)S(1)}, u32[32]{0:T(128)}, u32[]{:S(2)}) copy-start(u32[32]{0:T(128)} %constant.207) | copy-start | bytes 388
  261.2 9.9 %copy-start.4 = (f32[512]{0:T(512)S(1)}, f32[512]{0:T(512)}, u32[]{:S(2)}) copy-start(f32[512]{0:T(512)} %param.18) | copy-start | bytes 6148
  261.2 129.7 %copy-start.7 = (f32[2048]{0:T(1024)S(1)}, f32[2048]{0:T(1024)}, u32[]{:S(2)}) copy-start(f32[2048]{0:T(1024)} %param.17) | copy-start | bytes 24580
Sparse Core Ops, SparseCore 0:
  10.2 67.2 all-gather.6
  79.6 127.4 all-gather.8
  209.3 125.2 all-gather.12
  336.0 54.8 all-gather.10
